TPU v7x, 32 devices: a whole 2x2x4 slice. The times are simulated.
32 devices in a mesh: rep: 2 (over x), atom: 8 (over z, y), dir: 2 (over core).
Axes of the slice: x: 2, y: 2, z: 4, core: 2. Of those that a mesh axis runs over, the one named last changes fastest.
Arguments:
- positions: float32 [3, 16384], P(None, ('rep', 'atom')), parts along dimension 1, may hold values from -8 to 8
- queries: bfloat16 [16384, 256], P(('rep', 'atom')), parts along dimension 0, may hold values from -6 to 6
- keys: bfloat16 [16384, 256], P(('rep', 'atom')), parts along dimension 0, may hold values from -6 to 6
- values: bfloat16 [16384, 256], P(('rep', 'atom')), parts along dimension 0, may hold values from -6 to 6
- cotangent: bfloat16 [16384, 256], P(('rep', 'atom')), parts along dimension 0, may hold values from -6 to 6
- block_counts: int32 [16], P(('rep', 'atom')), parts along dimension 0, may hold values from 1 to 1024, 6144 in all
- dir_cos: float32 [86], P('dir'), may hold values from -1 to 1
- dir_phase: float32 [86], P('dir'), may hold values from -3.140625 to 3.140625
- dir_weight: float32 [86], P('dir'), may hold values from 0.01 to 0.1
- frequencies: float32 [128], replicated, may hold values from 0.05 to 1
Outputs:
- grad_queries: bfloat16 [16384, 256], P(('rep', 'atom')), parts along dimension 0
- grad_keys: bfloat16 [16384, 256], P(('rep', 'atom')), parts along dimension 0
- grad_values: bfloat16 [16384, 256], P(('rep', 'atom')), parts along dimension 0
There are 2 independent parts, one for each index of `rep`. A program takes and returns all parts, laid end to end along the dimension named above; an argument that names none is the same for every part. Nothing has to cross between parts.
Inputs may be any that keep to these rules, and one draw needn't show every extreme that they name: `block_counts`: atom slots of a block past its count are padding; the counts of all blocks sum to 6144.
All inputs are finite; a program needn't handle non-finite values.
Results may differ from a plain program's by a relative error of at most 0.0034.
Values may be sent and summed in bfloat16 or wider, within the bound.
No kernel may reach another device: no remote copies, remote signals or barrier semaphores. Data moves between devices by JAX's collectives and lax.ppermute only.
A program may use at most 192 MiB of HBM per device.

v0:
```python
import math

import jax
import jax.numpy as jnp
from jax import lax
from jax.sharding import PartitionSpec as P

HEADS = 4
HD = 64


def rotate(first, second, cosine, sine):
    return (first * cosine - second * sine, first * sine + second * cosine)


def unrotate(first, second, cosine, sine):
    return (first * cosine + second * sine, second * cosine - first * sine)


def body(
    positions,
    queries,
    keys,
    values,
    cotangent,
    block_counts,
    dir_cos,
    dir_phase,
    dir_weight,
    frequencies,
):
    half = HD // 2
    rows = queries.shape[0]
    width = queries.shape[1]
    local_dirs = dir_cos.shape[0]
    blk_rows = min(rows, 512)
    num_blocks = rows // blk_rows
    scale = 1.0 / (8.0 * math.sqrt(rows * lax.axis_size("atom")))
    row_mask = (jnp.arange(rows, dtype=jnp.int32) < block_counts[0]).astype(jnp.float32)
    sin_polar = jnp.sqrt(1.0 - dir_cos * dir_cos)
    directions = jnp.stack(
        [sin_polar * jnp.cos(dir_phase), sin_polar * jnp.sin(dir_phase), dir_cos], axis=0
    )
    freq = frequencies.reshape(HEADS, half)
    pos_blocks = positions.reshape(3, num_blocks, blk_rows).transpose(1, 0, 2)
    q_blocks = queries.reshape(num_blocks, blk_rows, width)
    k_blocks = keys.reshape(num_blocks, blk_rows, width)
    v_blocks = values.reshape(num_blocks, blk_rows, width)
    d_blocks = cotangent.reshape(num_blocks, blk_rows, width)
    m_blocks = row_mask.reshape(num_blocks, blk_rows)

    def rotated(pos_blk, q_blk, k_blk, m_blk):
        proj = jnp.sum(pos_blk[:, None, :] * directions[:, :, None], axis=0)
        theta = proj[:, :, None, None] * freq[None, None]
        cosine = jnp.cos(theta)
        sine = jnp.sin(theta)
        q_four = (
            q_blk.astype(jnp.float32).reshape(blk_rows, HEADS, 2, half) * m_blk[:, None, None, None]
        )
        k_four = (
            k_blk.astype(jnp.float32).reshape(blk_rows, HEADS, 2, half) * m_blk[:, None, None, None]
        )
        qa, qb = rotate(q_four[None, :, :, 0], q_four[None, :, :, 1], cosine, sine)
        ka, kb = rotate(k_four[None, :, :, 0], k_four[None, :, :, 1], cosine, sine)
        qrot = jnp.concatenate([qa, qb], axis=3).astype(jnp.bfloat16)
        krot = jnp.concatenate([ka, kb], axis=3).astype(jnp.bfloat16)
        return (qrot, krot, cosine, sine)

    def accumulate(carry, item):
        summ_acc, grad_acc = carry
        pos_blk, q_blk, k_blk, v_blk, d_blk, m_blk = item
        qrot, krot, cosine, sine = rotated(pos_blk, q_blk, k_blk, m_blk)
        v_three = v_blk.reshape(blk_rows, HEADS, HD)
        d_three = d_blk.reshape(blk_rows, HEADS, HD)
        summ_acc = summ_acc + jnp.einsum(
            "uahc,ahd->uhcd", krot, v_three, preferred_element_type=jnp.float32
        )
        grad_acc = grad_acc + jnp.einsum(
            "uahc,ahd->uhcd", qrot, d_three, preferred_element_type=jnp.float32
        )
        return ((summ_acc, grad_acc), None)

    empty = jnp.zeros((local_dirs, HEADS, HD, HD), jnp.float32)
    items = (pos_blocks, q_blocks, k_blocks, v_blocks, d_blocks, m_blocks)
    (summ_raw, grad_raw), unused = lax.scan(accumulate, (empty, empty), items)
    factor = (scale * dir_weight)[:, None, None, None]
    summ_part = factor * summ_raw
    grad_part = factor * grad_raw
    summ_sum, grad_sum = lax.psum((summ_part, grad_part), "atom")
    summary = summ_sum.astype(jnp.bfloat16)
    grad_summary = grad_sum.astype(jnp.bfloat16)

    def gradients(item):
        pos_blk, q_blk, k_blk, v_blk, d_blk, m_blk = item
        qrot, krot, cosine, sine = rotated(pos_blk, q_blk, k_blk, m_blk)
        v_three = v_blk.reshape(blk_rows, HEADS, HD)
        d_three = d_blk.reshape(blk_rows, HEADS, HD)
        dq_rot = jnp.einsum("ahd,uhcd->uahc", d_three, summary, preferred_element_type=jnp.float32)
        dk_rot = jnp.einsum(
            "ahd,uhcd->uahc", v_three, grad_summary, preferred_element_type=jnp.float32
        )
        qa2, qb2 = unrotate(dq_rot[..., :half], dq_rot[..., half:], cosine, sine)
        ka2, kb2 = unrotate(dk_rot[..., :half], dk_rot[..., half:], cosine, sine)
        grad_q = jnp.sum(jnp.concatenate([qa2, qb2], axis=3), axis=0).reshape(blk_rows, width)
        grad_k = jnp.sum(jnp.concatenate([ka2, kb2], axis=3), axis=0).reshape(blk_rows, width)
        grad_v = jnp.einsum(
            "uahc,uhcd->ahd", krot, grad_summary, preferred_element_type=jnp.float32
        ).reshape(blk_rows, width)
        return (grad_q, grad_k, grad_v)

    grad_q, grad_k, grad_v = lax.map(gradients, items)
    grad_q = grad_q.reshape(rows, width)
    grad_k = grad_k.reshape(rows, width)
    grad_v = grad_v.reshape(rows, width)
    col_mask = row_mask[:, None]
    grad_q, grad_k, grad_v = lax.psum((grad_q, grad_k, grad_v), "dir")
    return (
        (grad_q * col_mask).astype(jnp.bfloat16),
        (grad_k * col_mask).astype(jnp.bfloat16),
        (grad_v * col_mask).astype(jnp.bfloat16),
    )


def solution(mesh):
    in_specs = (
        P(None, ("rep", "atom")),
        P(("rep", "atom"), None),
        P(("rep", "atom"), None),
        P(("rep", "atom"), None),
        P(("rep", "atom"), None),
        P(("rep", "atom")),
        P("dir"),
        P("dir"),
        P("dir"),
        P(),
    )
    out_specs = (P(("rep", "atom"), None), P(("rep", "atom"), None), P(("rep", "atom"), None))
    return jax.shard_map(body, mesh=mesh, in_specs=in_specs, out_specs=out_specs, check_vma=False)
```

profile of v0, /device:TPU:0, one launch (start us, length us, event | category | flops | bytes accessed | tf_op | source)
XLA Modules:
  0.0 847.1 jit_solution(2837747684575133564)
XLA Ops:
  13.9 139.5 %while.28 = (s32[]{:T(128)}, f32[43,4,64,64]{2,3,0,1:T(8,128)}, f32[43,4,64,64]{2,3,0,1:T(8,128)}, bf16[2,512,256]{1,2,0:T(8,128)(2,1)S(1)}, bf16[2,512,256]{1,2...) while((s32[]{:T(128)}, f32[43,4,64,64]{2,3,0,1:T(8,128)}, ...), condition=%wide.region_2.3_spmd.clone, body=%wide.region_0.2_spmd.clone.sunk | while | flops 1539288576 | bytes 109517016 | solution.py:85
  17.8 47.7 %fusion.88 = (bf16[43,512,4,32]{1,3,0,2:T(8,128)(2,1)}, bf16[43,512,4,32]{1,3,0,2:T(8,128)(2,1)}, bf16[43,512,4,32]{1,3,0,2:T(8,128)(2,1)}, bf16[43,512,4,32]{1,3,0,2:T(8,128)(2,1)}) fusion(f32[512,4,32]{0,2,1:T(8,128)S(1)} %get-tuple-element.524, f32[512,4,32]{0,2,1:T(8,128)S(1)} %get-tuple-element.525, f32[4,32]{1,0:T(4,128)S(1)} %mul.577, ...), kind=kLoop, calls=%fused_computation.58.clone.1 | loop fusion | flops 47906816 | bytes 23681536 | tf_op jit(solution)/shard_map/convert.2
  65.5 9.6 %bitcast_add_fusion.5 = f32[43,4,64,64]{2,3,0,1:T(8,128)} fusion(f32[43,4,64,64]{2,3,0,1:T(8,128)} %get-tuple-element.549, pred[]{:T(512)S(6)} %compare.3, bf16[512,4,64,1]{0,2,3,1:T(8,128)(2,1)S(1)} %bitcast.150, bf16[43,512,4,32]{1,3,0,2:T(8,128)(2,1)} %get-tuple-element.532, bf16[43,512,4,32]{1,3,0,2:T(8,128)(2,1)} %get-tuple-element.533), kind=kOutput, calls=%fused_computation.69.clone.1 | convolution fusion | flops 745373696 | bytes 17170432 | tf_op jit(solution)/shard_map/while/body/eval_jaxpr/uahc,ahd->uhcd/dot_general | solution.py:78
  75.2 7.0 bitcast_add_fusion.4
  86.0 47.7 %fusion.88 = (bf16[43,512,4,32]{1,3,0,2:T(8,128)(2,1)}, bf16[43,512,4,32]{1,3,0,2:T(8,128)(2,1)}, bf16[43,512,4,32]{1,3,0,2:T(8,128)(2,1)}, bf16[43,512,4,32]{1,3,0,2:T(8,128)(2,1)}) fusion(f32[512,4,32]{0,2,1:T(8,128)S(1)} %get-tuple-element.524, f32[512,4,32]{0,2,1:T(8,128)S(1)} %get-tuple-element.525, f32[4,32]{1,0:T(4,128)S(1)} %mul.577, ...), kind=kLoop, calls=%fused_computation.58.clone.1 | loop fusion | flops 47906816 | bytes 23681536 | tf_op jit(solution)/shard_map/convert.2
  133.7 10.5 %bitcast_add_fusion.5 = f32[43,4,64,64]{2,3,0,1:T(8,128)} fusion(f32[43,4,64,64]{2,3,0,1:T(8,128)} %get-tuple-element.549, pred[]{:T(512)S(6)} %compare.3, bf16[512,4,64,1]{0,2,3,1:T(8,128)(2,1)S(1)} %bitcast.150, bf16[43,512,4,32]{1,3,0,2:T(8,128)(2,1)} %get-tuple-element.532, bf16[43,512,4,32]{1,3,0,2:T(8,128)(2,1)} %get-tuple-element.533), kind=kOutput, calls=%fused_computation.69.clone.1 | convolution fusion | flops 745373696 | bytes 17170432 | tf_op jit(solution)/shard_map/while/body/eval_jaxpr/uahc,ahd->uhcd/dot_general | solution.py:78
  144.6 8.7 %bitcast_add_fusion.4 = f32[43,4,64,64]{2,3,0,1:T(8,128)} fusion(f32[43,4,64,64]{2,3,0,1:T(8,128)} %get-tuple-element.548, pred[]{:T(512)S(6)} %compare.3, bf16[512,4,64,1]{0,2,3,1:T(8,128)(2,1)S(1)} %bitcast.149, bf16[43,512,4,32]{1,3,0,2:T(8,128)(2,1)S(1)} %copy-done, bf16[43,512,4,32]{1,3,0,2:T(8,128)(2,1)S(1)} %copy-done.1), kind=kOutput, calls=%fused_computation.70.clone.1 | convolution fusion | flops 745373696 | bytes 17170432 | tf_op jit(solution)/shard_map/while/body/eval_jaxpr/uahc,ahd->uhcd/dot_general | solution.py:75
  153.3 11.5 %broadcast_multiply_fusion = (f32[43,4,64,64]{2,3,0,1:T(8,128)}, f32[43,4,64,64]{2,3,0,1:T(8,128)}) fusion(f32[43,4,64,64]{2,3,0,1:T(8,128)} %get-tuple-element.131, f32[43]{0:T(128)S(1)} %broadcast_multiply_fusion.2, f32[43,4,64,64]{2,3,0,1:T(8,128)} %get-tuple-element.130), kind=kLoop, calls=%fused_computation.86 | loop fusion | flops 1409024 | bytes 11272364 | tf_op jit(solution)/shard_map/mul | solution.py:88
  164.9 437.5 %all-reduce.6 = (bf16[43,4,64,64]{2,3,0,1:T(8,128)(2,1)}, bf16[43,4,64,64]{2,3,0,1:T(8,128)(2,1)}) all-reduce(f32[43,4,64,64]{2,3,0,1:T(8,128)} %get-tuple-element.343, f32[43,4,64,64]{2,3,0,1:T(8,128)} %get-tuple-element.342), channel_id=1, replica_groups=mesh['rep'=2,'atom'=8,'dir'=2] {'atom'}, use_global_device_ids=true, to_apply=%region_3.4 | all-reduce | flops 1409024 | bytes 8454144 | tf_op jit(solution)/shard_map/psum | solution.py:89
  602.4 3.3 copy.47
  605.7 209.4 %while.27 = (s32[]{:T(128)}, f32[2,512,256]{2,1,0:T(8,128)}, f32[2,512,256]{2,1,0:T(8,128)}, f32[2,512,256]{2,1,0:T(8,128)}, bf16[2,512,256]{1,2,0:T(8,128)(2,1)...) while((s32[]{:T(128)}, f32[2,512,256]{2,1,0:T(8,128)}, ...), condition=%wide.region_9.10_spmd, body=%wide.region_5.9_spmd.sunk | while | flops 2268638720 | bytes 221748416 | solution.py:111
  607.8 11.2 %convolution_bitcast_fusion.5 = f32[43,512,4,64]{1,3,0,2:T(8,128)} fusion(bf16[512,4,64,1]{0,2,3,1:T(8,128)(2,1)S(1)} %bitcast.143, bf16[43,4,64,64]{2,3,0,1:T(8,128)(2,1)} %get-tuple-element.611), kind=kOutput, calls=%fused_computation.28.clone.1 | convolution fusion | flops 721420288 | bytes 24215552 | tf_op jit(solution)/shard_map/while/body/eval_jaxpr/ahd,uhcd->uahc/dot_general | solution.py:99
  619.1 9.1 %convolution_bitcast_fusion.4 = f32[43,512,4,64]{1,3,0,2:T(8,128)} fusion(bf16[512,4,64,1]{0,2,3,1:T(8,128)(2,1)S(1)} %bitcast.144, bf16[43,4,64,64]{3,2,0,1:T(8,128)(2,1)S(1)} %get-tuple-element.606), kind=kOutput, calls=%fused_computation.29.clone.1 | convolution fusion | flops 721420288 | bytes 24215552 | tf_op jit(solution)/shard_map/while/body/eval_jaxpr/ahd,uhcd->uahc/dot_general | solution.py:98
  628.4 53.8 %fusion.82 = (bf16[43,512,4,32]{1,3,0,2:T(8,128)(2,1)}, bf16[43,512,4,32]{1,3,0,2:T(8,128)(2,1)}, f32[43,512,4,32]{1,3,0,2:T(8,128)}, f32[43,512,4,32]{1,3,0,2:T...) fusion(f32[512,4,32]{0,2,1:T(8,128)S(1)} %get-tuple-element.501, ...), kind=kLoop, calls=%fused_computation.21.clone.1 | loop fusion | flops 59179008 | bytes 102062592 | tf_op jit(solution)/shard_map/convert.7
  682.2 3.8 maximum_reduce_fusion.5
  687.3 7.0 fusion.83
  698.4 9.1 %maximum_reduce_fusion.4 = f32[512,4,64]{0,2,1:T(8,128)S(1)} fusion(f32[43,512,4,32]{1,3,0,2:T(8,128)} %get-tuple-element.503, f32[43,512,4,32]{1,3,0,2:T(8,128)} %get-tuple-element.504), kind=kLoop, calls=%fused_computation.clone.1 | loop fusion | flops 11141120 | bytes 23068672 | tf_op jit(solution)/shard_map/while/body/eval_jaxpr/reduce_sum | solution.py:104
  712.5 11.2 %convolution_bitcast_fusion.5 = f32[43,512,4,64]{1,3,0,2:T(8,128)} fusion(bf16[512,4,64,1]{0,2,3,1:T(8,128)(2,1)S(1)} %bitcast.143, bf16[43,4,64,64]{2,3,0,1:T(8,128)(2,1)} %get-tuple-element.611), kind=kOutput, calls=%fused_computation.28.clone.1 | convolution fusion | flops 721420288 | bytes 24215552 | tf_op jit(solution)/shard_map/while/body/eval_jaxpr/ahd,uhcd->uahc/dot_general | solution.py:99
  723.8 9.1 %convolution_bitcast_fusion.4 = f32[43,512,4,64]{1,3,0,2:T(8,128)} fusion(bf16[512,4,64,1]{0,2,3,1:T(8,128)(2,1)S(1)} %bitcast.144, bf16[43,4,64,64]{3,2,0,1:T(8,128)(2,1)S(1)} %get-tuple-element.606), kind=kOutput, calls=%fused_computation.29.clone.1 | convolution fusion | flops 721420288 | bytes 24215552 | tf_op jit(solution)/shard_map/while/body/eval_jaxpr/ahd,uhcd->uahc/dot_general | solution.py:98
  733.0 53.8 %fusion.82 = (bf16[43,512,4,32]{1,3,0,2:T(8,128)(2,1)}, bf16[43,512,4,32]{1,3,0,2:T(8,128)(2,1)}, f32[43,512,4,32]{1,3,0,2:T(8,128)}, f32[43,512,4,32]{1,3,0,2:T...) fusion(f32[512,4,32]{0,2,1:T(8,128)S(1)} %get-tuple-element.501, ...), kind=kLoop, calls=%fused_computation.21.clone.1 | loop fusion | flops 59179008 | bytes 102062592 | tf_op jit(solution)/shard_map/convert.7
  786.9 3.8 maximum_reduce_fusion.5
  791.9 7.0 fusion.83
  803.1 9.1 %maximum_reduce_fusion.4 = f32[512,4,64]{0,2,1:T(8,128)S(1)} fusion(f32[43,512,4,32]{1,3,0,2:T(8,128)} %get-tuple-element.503, f32[43,512,4,32]{1,3,0,2:T(8,128)} %get-tuple-element.504), kind=kLoop, calls=%fused_computation.clone.1 | loop fusion | flops 11141120 | bytes 23068672 | tf_op jit(solution)/shard_map/while/body/eval_jaxpr/reduce_sum | solution.py:104
  815.2 21.8 %all-reduce.5.cloned.1.call-done = (f32[1024,256]{1,0:T(8,128)}, f32[1024,256]{1,0:T(8,128)}, f32[1024,256]{1,0:T(8,128)}) async-done(((f32[1024,256]{1,0:T(8,128)}, f32[1024,256]{1,0:T(8,128)}, f32[1024,256]{1,0:T(8,128)}), (f32[1024,256]{1,0:T(8,128)}, f32[1024,256]{1,0:T(8,128)}, f32[1024,256]{1,0:T(8,128)})) %all-reduce.5.cloned.1.call-update) | async-done | bytes 3145744 | tf_op jit(solution)/shard_map/psum | solution.py:116
  (88 shorter events, 38.4 us)
Async XLA Ops:
  7.2 829.9 %all-reduce.5.cloned.1.call-start = ((), (), s32[]{:S(2)}) async-start(), calls=%async_computation | async-start | bytes 6291456 | tf_op jit(solution)/shard_map/psum | solution.py:116
  13.9 139.5 %copy-start.7 = (f32[43]{0:T(128)S(1)}, f32[43]{0:T(128)}, u32[]{:S(2)}) copy-start(f32[43]{0:T(128)} %param.22) | copy-start | bytes 520
  65.5 9.7 %copy-start = (bf16[43,512,4,32]{1,3,0,2:T(8,128)(2,1)S(1)}, bf16[43,512,4,32]{1,3,0,2:T(8,128)(2,1)}, u32[]{:S(2)}) copy-start(bf16[43,512,4,32]{1,3,0,2:T(8,128)(2,1)} %get-tuple-element.529) | copy-start | bytes 16908292 | tf_op jit(solution)/shard_map/while
  65.5 9.7 %copy-start.1 = (bf16[43,512,4,32]{1,3,0,2:T(8,128)(2,1)S(1)}, bf16[43,512,4,32]{1,3,0,2:T(8,128)(2,1)}, u32[]{:S(2)}) copy-start(bf16[43,512,4,32]{1,3,0,2:T(8,128)(2,1)} %get-tuple-element.530) | copy-start | bytes 16908292 | tf_op jit(solution)/shard_map/while
  133.7 10.5 %copy-start = (bf16[43,512,4,32]{1,3,0,2:T(8,128)(2,1)S(1)}, bf16[43,512,4,32]{1,3,0,2:T(8,128)(2,1)}, u32[]{:S(2)}) copy-start(bf16[43,512,4,32]{1,3,0,2:T(8,128)(2,1)} %get-tuple-element.529) | copy-start | bytes 16908292 | tf_op jit(solution)/shard_map/while
  133.7 10.9 %copy-start.1 = (bf16[43,512,4,32]{1,3,0,2:T(8,128)(2,1)S(1)}, bf16[43,512,4,32]{1,3,0,2:T(8,128)(2,1)}, u32[]{:S(2)}) copy-start(bf16[43,512,4,32]{1,3,0,2:T(8,128)(2,1)} %get-tuple-element.530) | copy-start | bytes 16908292 | tf_op jit(solution)/shard_map/while
  153.3 11.6 %copy-start.2 = (bf16[2,512,256]{1,2,0:T(8,128)(2,1)}, bf16[2,512,256]{1,2,0:T(8,128)(2,1)S(1)}, u32[]{:S(2)}) copy-start(bf16[2,512,256]{1,2,0:T(8,128)(2,1)S(1)} %get-tuple-element.621) | copy-start | bytes 1572868
  153.3 11.6 %copy-start.3 = (bf16[2,512,256]{1,2,0:T(8,128)(2,1)}, bf16[2,512,256]{1,2,0:T(8,128)(2,1)S(1)}, u32[]{:S(2)}) copy-start(bf16[2,512,256]{1,2,0:T(8,128)(2,1)S(1)} %get-tuple-element.622) | copy-start | bytes 1572868
  164.9 440.9 %copy-start.5 = (f32[2,3,512]{2,1,0:T(4,128)S(1)}, f32[2,3,512]{2,1,0:T(4,128)}, u32[]{:S(2)}) copy-start(f32[2,3,512]{2,1,0:T(4,128)} %get-tuple-element.631) | copy-start | bytes 36868
  164.9 440.9 %copy-start.6 = (f32[128]{0:T(128)S(1)}, f32[128]{0:T(128)}, u32[]{:S(2)}) copy-start(f32[128]{0:T(128)} %get-tuple-element.634) | copy-start | bytes 1540
  607.8 11.2 %copy-start.4 = (bf16[2,512,256]{1,2,0:T(8,128)(2,1)S(1)}, bf16[2,512,256]{1,2,0:T(8,128)(2,1)}, u32[]{:S(2)}) copy-start(bf16[2,512,256]{1,2,0:T(8,128)(2,1)} %get-tuple-element.605) | copy-start | bytes 1572868 | tf_op jit(solution)/shard_map/while
  712.5 11.2 %copy-start.4 = (bf16[2,512,256]{1,2,0:T(8,128)(2,1)S(1)}, bf16[2,512,256]{1,2,0:T(8,128)(2,1)}, u32[]{:S(2)}) copy-start(bf16[2,512,256]{1,2,0:T(8,128)(2,1)} %get-tuple-element.605) | copy-start | bytes 1572868 | tf_op jit(solution)/shard_map/while
Sparse Core Ops, SparseCore 0:
  815.3 21.6 all-reduce.4
where the time goes:
time: 848 us; the launch traced here: 847 us
  blocking collectives  438 us (52%)
  other arithmetic  246 us (29%)
  matrix products  90.4 us (11%)
  local copies, waits for them, and re-layouts  36.3 us (4%)
  waiting for transfers between devices  21.9 us (3%)
  between operations  14.8 us (2%)
    psum x1, blocking collectives, body(): summ_sum, grad_sum = lax.psum((summ_part, grad_part), 'atom')  438 us
    another operation x7, other arithmetic  203 us
    dot_general x2, matrix products, gradients(): jnp.einsum('ahd,uhcd->uahc', v_three, grad_summary, preferred_element_typ...  22.4 us
    psum x1, waiting for transfers between devices, body(): grad_q, grad_k, grad_v = lax.psum((grad_q, grad_k, grad_v), 'dir')  21.8 us
    dot_general x2, matrix products, accumulate(): jnp.einsum('uahc,ahd->uhcd', qrot, d_three, preferred_element_type=jnp.fl...  20.1 us
    reduce_sum x2, other arithmetic, gradients(): jnp.sum(jnp.concatenate([qa2, qb2], axis=3), axis=0)  18.3 us
    dot_general x2, matrix products, gradients(): jnp.einsum('ahd,uhcd->uahc', d_three, summary, preferred_element_type=jnp...  18.2 us
  transfers between devices with their start and end apart: 1, of which 1 were waited for; matrix products, arithmetic and copies ran while one was open for 0% of the time, Pallas kernels for 0%

commit v1 on v0

v1 whole, which is shorter than its diff:
```python
import functools
import math

import jax
import jax.numpy as jnp
import numpy as np
from jax import lax
from jax.experimental import pallas as pl
from jax.experimental.pallas import tpu as pltpu
from jax.sharding import PartitionSpec as P

HEADS = 4
HD = 64
HALF = 32
GROUP = 4
NODES = 16
SHARDS = 8
CHUNKS = (2, 3, 3, 3)
F32 = jnp.float32
BF16 = jnp.bfloat16
F16 = jnp.float16

_NODE = np.cos((np.arange(NODES) + 0.5) * np.pi / (2 * NODES)).astype(np.float32)


def _fit(func, terms):
    z = 0.125 * (1 - np.cos((np.arange(256) + 0.5) * np.pi / 256))
    cheb = np.polynomial.chebyshev.Chebyshev.fit(z, func(z), terms - 1, domain=[0, 0.25])
    return [float(c) for c in cheb.convert(kind=np.polynomial.Polynomial).coef]


_SIN = _fit(lambda z: np.sin(2 * np.pi * np.sqrt(z)) / np.sqrt(z), 7)
_COS = _fit(lambda z: np.cos(2 * np.pi * np.sqrt(z)), 7)


def horner(coef, z):
    acc = coef[-1] * z + coef[-2]
    for c in coef[-3::-1]:
        acc = acc * z + c
    return acc


def pair_coefs(frequencies):
    node = jnp.asarray(_NODE)
    n64 = _NODE.astype(np.float64)
    den = n64[:, None] ** 2 - n64[None, :] ** 2
    np.fill_diagonal(den, 1.0)
    inv = jnp.asarray((1.0 / den).astype(np.float32))
    f = frequencies[:, None]
    num = (f - node) * (f + node)
    fac = jnp.where(jnp.eye(NODES, dtype=bool)[None], 1.0, num[:, None, :] * inv[None])
    cosine = jnp.prod(fac, axis=2)
    sine = cosine * (f / node)
    zero = jnp.zeros_like(cosine)
    full = jnp.concatenate(
        [jnp.concatenate([cosine, zero], 1), jnp.concatenate([zero, sine], 1)], 0
    )
    one = lax.reduce_precision(full, 8, 7)
    two = lax.reduce_precision(full - one, 8, 7)
    three = full - one - two
    return jnp.concatenate([one, two, three, one, two, one], 1).astype(BF16)


def store_features(feat_ref, node_ref, proj_row):
    turns = node_ref[...] * proj_row
    turns = turns - jnp.round(turns)
    z = turns * turns
    full = jnp.concatenate([horner(_COS, z), turns * horner(_SIN, z)], axis=0)
    one = full.astype(BF16)
    rest = full - one.astype(F32)
    two = rest.astype(BF16)
    three = (rest - two.astype(F32)).astype(BF16)
    feat_ref[...] = jnp.concatenate([one, one, one, two, two, three], axis=0)


def pass_one(rows, tile, proj_ref, node_ref, coef_ref, qt_ref, kt_ref, w_ref, out_ref, feat_ref, rot_ref):
    for u in range(GROUP):
        store_features(feat_ref, node_ref, proj_ref[0, u : u + 1, :])
        lo = slice(u * HD, u * HD + HALF)
        hi = slice(u * HD + HALF, (u + 1) * HD)
        for t in range(rows // tile):
            at = slice(t * tile, (t + 1) * tile)
            trig = jnp.dot(coef_ref[...], feat_ref[:, at], preferred_element_type=F32)
            for h in range(HEADS):
                c = trig[h * HALF : (h + 1) * HALF]
                s = trig[128 + h * HALF : 128 + (h + 1) * HALF]
                for i, src in enumerate((kt_ref, qt_ref)):
                    to = slice(i * rows + t * tile, i * rows + (t + 1) * tile)
                    a = src[h * HD : h * HD + HALF, at]
                    b = src[h * HD + HALF : (h + 1) * HD, at]
                    rot_ref[h, lo, to] = (a * c - b * s).astype(BF16)
                    rot_ref[h, hi, to] = (a * s + b * c).astype(BF16)
    for h in range(HEADS):
        res = jnp.dot(rot_ref[h], w_ref[h], preferred_element_type=F32)
        for u in range(GROUP):
            out_ref[2 * h, u] = res[u * HD : u * HD + HALF]
            out_ref[2 * h + 1, u] = res[u * HD + HALF : (u + 1) * HD]


def pass_two(rows, tile, first_ref, proj_ref, node_ref, coef_ref, kt_ref, rhs_ref, sg_ref, q_in, k_in, v_in, gq_ref, gk_ref, gv_ref, feat_ref, rot_ref, d_ref):
    @pl.when(pl.program_id(0) == 0)
    def _():
        gq_ref[...] = q_in[...]
        gk_ref[...] = k_in[...]
        gv_ref[...] = v_in[...]

    for u in range(GROUP):
        store_features(feat_ref.at[u], node_ref, proj_ref[0, u : u + 1, :])
    gs = []
    for h in range(HEADS):
        parts = []
        for u in range(GROUP):
            parts.append(sg_ref[lax.rem(2 * h + first_ref[0], SHARDS), u])
            parts.append(sg_ref[lax.rem(2 * h + 1 + first_ref[0], SHARDS), u])
        sg = jnp.concatenate(parts, axis=0)
        d_ref[h] = jnp.dot(sg, rhs_ref[h], preferred_element_type=F32)
        gs.append(jnp.transpose(sg[:, HD:].astype(F32)).astype(BF16))
    for t in range(rows // tile):
        at = slice(t * tile, (t + 1) * tile)
        at2 = slice(rows + t * tile, rows + (t + 1) * tile)
        for u in range(GROUP):
            trig = jnp.dot(coef_ref[...], feat_ref[u, :, at], preferred_element_type=F32)
            ulo = slice(u * HD, u * HD + HALF)
            uhi = slice(u * HD + HALF, (u + 1) * HD)
            for h in range(HEADS):
                c = trig[h * HALF : (h + 1) * HALF]
                s = trig[128 + h * HALF : 128 + (h + 1) * HALF]
                lo = slice(h * HD, h * HD + HALF)
                hi = slice(h * HD + HALF, (h + 1) * HD)
                a = kt_ref[lo, at]
                b = kt_ref[hi, at]
                rot_ref[h, ulo, at] = (a * c - b * s).astype(BF16)
                rot_ref[h, uhi, at] = (a * s + b * c).astype(BF16)
                a = d_ref[h, ulo, at]
                b = d_ref[h, uhi, at]
                gq_ref[lo, at] += a * c + b * s
                gq_ref[hi, at] += b * c - a * s
                a = d_ref[h, ulo, at2]
                b = d_ref[h, uhi, at2]
                gk_ref[lo, at] += a * c + b * s
                gk_ref[hi, at] += b * c - a * s
    for h in range(HEADS):
        gv_ref[h * HD : (h + 1) * HD, :] += jnp.dot(gs[h], rot_ref[h], preferred_element_type=F32)


def whole(shape):
    return pl.BlockSpec(shape, lambda g: (0,) * len(shape))


def call_one(proj, node, coef, qt, kt, w, tile=256):
    steps, unused, rows = proj.shape
    nd = steps * GROUP
    return pl.pallas_call(
        functools.partial(pass_one, rows, tile),
        name="pass_one",
        grid=(steps,),
        in_specs=[
            pl.BlockSpec((1, GROUP, rows), lambda g: (g, 0, 0)),
            whole(node.shape),
            whole(coef.shape),
            whole(qt.shape),
            whole(kt.shape),
            whole(w.shape),
        ],
        out_specs=pl.BlockSpec((SHARDS, GROUP, HALF, 128), lambda g: (0, g, 0, 0)),
        out_shape=jax.ShapeDtypeStruct((SHARDS, nd, HALF, 128), F32),
        scratch_shapes=[
            pltpu.VMEM((192, rows), BF16),
            pltpu.VMEM((HEADS, GROUP * HD, 2 * rows), BF16),
        ],
        compiler_params=pltpu.CompilerParams(vmem_limit_bytes=56 << 20),
    )(proj, node, coef, qt, kt, w)


def call_two(first, proj, node, coef, kt, rhs, sg, grads, tile=128):
    steps, unused, rows = proj.shape
    width = HEADS * HD
    out = jax.ShapeDtypeStruct((width, rows), F32)
    return pl.pallas_call(
        functools.partial(pass_two, rows, tile),
        name="pass_two",
        grid=(steps,),
        in_specs=[
            pl.BlockSpec(memory_space=pltpu.SMEM),
            pl.BlockSpec((1, GROUP, rows), lambda g: (g, 0, 0)),
            whole(node.shape),
            whole(coef.shape),
            whole(kt.shape),
            whole(rhs.shape),
            pl.BlockSpec((SHARDS, GROUP, HALF, 128), lambda g: (0, g, 0, 0)),
        ]
        + [whole((width, rows))] * 3,
        out_specs=[whole((width, rows))] * 3,
        out_shape=[out] * 3,
        scratch_shapes=[
            pltpu.VMEM((GROUP, 192, rows), BF16),
            pltpu.VMEM((HEADS, GROUP * HD, rows), BF16),
            pltpu.VMEM((HEADS, GROUP * HD, 2 * rows), F32),
        ],
        input_output_aliases={7: 0, 8: 1, 9: 2},
        compiler_params=pltpu.CompilerParams(vmem_limit_bytes=60 << 20),
    )(first, proj, node, coef, kt, rhs, sg, *grads)


RING = (0, 2, 4, 6, 7, 5, 3, 1)


class Ring:
    def __init__(self, axis, count):
        self.axis = axis
        self.count = count
        where = np.argsort(np.array(RING)).astype(np.int32)
        self.me = jnp.asarray(where)[lax.axis_index(axis)]
        self.up_pairs = [(RING[i], RING[(i + 1) % count]) for i in range(count)]
        self.down_pairs = [(b, a) for a, b in self.up_pairs]

    def up(self, x):
        return lax.ppermute(x, self.axis, self.up_pairs)

    def down(self, x):
        return lax.ppermute(x, self.axis, self.down_pairs)

    def at(self, x, ahead):
        index = lax.rem(self.me + (ahead + self.count), self.count)
        return lax.dynamic_index_in_dim(x, index, 0, keepdims=False)

    def scatter_sum(self, x, gain):
        half = x.shape[1] // 2
        own = lambda d: self.at(x, d) * gain
        last = None
        for step in range(1, 5):
            ahead = 5 - step
            up, down = own(ahead), own(-ahead)
            if step == 1:
                up, down = up[:half], down[half:]
            elif step == 2:
                up = jnp.concatenate([up[:half] + last[0], up[half:]], 0)
                down = jnp.concatenate([down[:half], down[half:] + last[1]], 0)
            else:
                up, down = up + last[0], down + last[1]
            got = self.up(up.astype(F16)), self.down(down.astype(F16))
            last = [g.astype(F32) for g in got]
        return own(0) + last[0] + last[1]

    def gather(self, x):
        half = x.shape[0] // 2
        up, down = x, x
        below, above = [], []
        for step in range(3):
            up, down = self.up(up), self.down(down)
            below.append(up)
            above.append(down)
        far = jnp.concatenate([self.up(up[:half]), self.down(down[half:])], 0)
        return jnp.stack([far] + below[::-1] + [x] + above, 0)


def body(
    positions,
    queries,
    keys,
    values,
    cotangent,
    block_counts,
    dir_cos,
    dir_phase,
    dir_weight,
    frequencies,
):
    rows, width = queries.shape
    n_atom = lax.axis_size("atom")
    scale = 1.0 / (8.0 * math.sqrt(rows * n_atom))
    local = dir_cos.shape[0]
    groups = -(-local // GROUP)
    pad = groups * GROUP - local
    sizes = CHUNKS if sum(CHUNKS) == groups else (groups,)

    sin_polar = jnp.sqrt(1.0 - dir_cos * dir_cos)
    directions = jnp.stack(
        [sin_polar * jnp.cos(dir_phase), sin_polar * jnp.sin(dir_phase), dir_cos], axis=0
    )
    proj = jnp.sum(positions[:, None, :] * directions[:, :, None], axis=0)
    proj = jnp.pad(proj, ((0, pad), (0, 0))).reshape(groups, GROUP, rows)
    factor = jnp.pad(scale * dir_weight, (0, pad))
    node = jnp.asarray((_NODE.astype(np.float64) / (2 * np.pi)).astype(np.float32))[:, None]
    coef = pair_coefs(frequencies)
    mask = (jnp.arange(rows, dtype=jnp.int32) < block_counts[0]).astype(F32)
    qt = (queries.astype(F32) * mask[:, None]).T
    kt = (keys.astype(F32) * mask[:, None]).T
    vh = values.reshape(rows, HEADS, HD).transpose(1, 0, 2)
    ch = cotangent.reshape(rows, HEADS, HD).transpose(1, 0, 2)
    zero = jnp.zeros_like(vh)
    w = jnp.concatenate(
        [jnp.concatenate([vh, zero], 2), jnp.concatenate([zero, ch], 2)], 1
    )
    vt = values.T.reshape(HEADS, HD, rows)
    ct = cotangent.T.reshape(HEADS, HD, rows)
    zero = jnp.zeros_like(vt)
    rhs = jnp.concatenate(
        [jnp.concatenate([ct, zero], 2), jnp.concatenate([zero, vt], 2)], 1
    )

    edges = np.cumsum((0,) + tuple(sizes))
    spans = [(int(a), int(b)) for a, b in zip(edges[:-1], edges[1:])]
    parts = [call_one(proj[a:b], node, coef, qt, kt, w) for a, b in spans]

    if n_atom == SHARDS:
        ring = Ring("atom", n_atom)
        peak = lambda x: jnp.max(jnp.abs(x.astype(F32)).reshape(rows, HEADS, HD), axis=(0, 2))
        bound = jnp.stack([peak(keys) * peak(values), peak(queries) * peak(cotangent)], 1)
        bound = lax.psum(bound, "atom") * (1.5 * rows)
        gain = jnp.exp2(jnp.floor(jnp.log2(60000.0 / jnp.maximum(bound, 1e-30))))
        gain = jnp.repeat(gain, HD, axis=1)
        gain = jnp.repeat(gain, 2, axis=0)
        sums = []
        for (a, b), part in zip(spans, parts):
            scaled = part * gain[:, None, None, :]
            total = ring.scatter_sum(scaled, 1.0)
            mine = lax.dynamic_index_in_dim(gain, ring.me, 0, keepdims=False)
            fac = factor[a * GROUP : b * GROUP]
            total = total * (fac[:, None, None] * (1.0 / mine)[None, None, :])
            sums.append(ring.gather(total.astype(BF16)))
        first = (SHARDS + 4 - ring.me).reshape(1)
    else:
        sums = []
        for (a, b), part in zip(spans, parts):
            fac = factor[a * GROUP : b * GROUP]
            sums.append(lax.psum(part * fac[None, :, None, None], "atom").astype(BF16))
        first = jnp.zeros((1,), jnp.int32)

    grads = [jnp.zeros((width, rows), F32)] * 3
    for (a, b), sg in zip(spans, sums):
        grads = call_two(first, proj[a:b], node, coef, kt, rhs, sg, grads)
    outs = []
    for g in grads:
        other = lax.ppermute(g, "dir", [(0, 1), (1, 0)])
        outs.append(((g + other) * mask[None, :]).astype(BF16).T)
    return tuple(outs)


def solution(mesh):
    in_specs = (
        P(None, ("rep", "atom")),
        P(("rep", "atom"), None),
        P(("rep", "atom"), None),
        P(("rep", "atom"), None),
        P(("rep", "atom"), None),
        P(("rep", "atom")),
        P("dir"),
        P("dir"),
        P("dir"),
        P(),
    )
    out_specs = (P(("rep", "atom"), None), P(("rep", "atom"), None), P(("rep", "atom"), None))
    return jax.shard_map(body, mesh=mesh, in_specs=in_specs, out_specs=out_specs, check_vma=False)
```

time: 848 us -> 298 us (0.35)
  blocking collectives: 438 us -> 23.3 us
  other arithmetic: 246 us -> 24.8 us
  Pallas kernels: 0 us -> 118 us
  matrix products: 90.4 us -> 0 us
  starting transfers between devices: 0.04 us -> 66.7 us
  local copies, waits for them, and re-layouts: 36.3 us -> 26.1 us
    psum x1, blocking collectives: 438 us -> 23.3 us  [body(): bound = lax.psum(bound, 'atom') * (1.5 * rows)]
    another operation x7 -> x6, other arithmetic: 203 us -> 2.9 us
    pallas_call x0 -> x8, Pallas kernels: none -> 118 us  [the longest x4 75.9 us: call_two(): pl.pallas_call(functools.partial(pass_two, rows, tile), name='pass_two',...]
    dot_general x10 -> x0, matrix products: 90.4 us -> none  [the longest x2 22.4 us: gradients(): jnp.einsum('ahd,uhcd->uahc', v_three, grad_summary, preferred_element_typ...]
    ppermute x0 -> x67, starting transfers between devices: none -> 66.7 us  [the longest x32 47.5 us: down(): return lax.ppermute(x, self.axis, self.down_pairs)]
    reduce_sum x8 -> x1, other arithmetic: 26.3 us -> 0.11 us  [body(): proj = jnp.sum(positions[:, None, :] * directions[:, :, None], axis=0)]
    ppermute x0 -> x67, waiting for transfers between devices: none -> 25.6 us  [the longest x32 10.6 us: down(): return lax.ppermute(x, self.axis, self.down_pairs)]
    psum x1 -> x0, waiting for transfers between devices: 21.8 us -> none  [body(): grad_q, grad_k, grad_v = lax.psum((grad_q, grad_k, grad_v), 'dir')]
  transfers between devices with their start and end apart: 1 -> 67, of which waited for: 1 -> 16; matrix products, arithmetic and copies ran while one was open for 0% -> 8% of each run, Pallas kernels for 0% -> 8%
where the time goes in v1:
time: 298 us; the launch traced here: 294 us
  Pallas kernels  118 us (40%)
  starting transfers between devices  66.7 us (22%)
  local copies, waits for them, and re-layouts  26.1 us (9%)
  waiting for transfers between devices  25.6 us (9%)
  other arithmetic  24.8 us (8%)
  blocking collectives  23.3 us (8%)
  between operations  9.3 us (3%)
    pallas_call x4, Pallas kernels, call_two(): pl.pallas_call(functools.partial(pass_two, rows, tile), name='pass_two',...  75.9 us
    ppermute x32, starting transfers between devices, down(): return lax.ppermute(x, self.axis, self.down_pairs)  47.5 us
    pallas_call x4, Pallas kernels, call_one(): pl.pallas_call(functools.partial(pass_one, rows, tile), name='pass_one',...  42.3 us
    psum x1, blocking collectives, body(): bound = lax.psum(bound, 'atom') * (1.5 * rows)  23.3 us
    ppermute x32, starting transfers between devices, up(): return lax.ppermute(x, self.axis, self.up_pairs)  18.6 us
    ppermute x32, waiting for transfers between devices, down(): return lax.ppermute(x, self.axis, self.down_pairs)  10.6 us
    ppermute x32, waiting for transfers between devices, up(): return lax.ppermute(x, self.axis, self.up_pairs)  9.63 us
    unnamed x77, local copies, waits for them, and re-layouts  9.24 us
  transfers between devices with their start and end apart: 67, of which 16 were waited for; matrix products, arithmetic and copies ran while one was open for 8% of the time, Pallas kernels for 8%

profile of v1, /device:TPU:0, one launch (start us, length us, event | category | flops | bytes accessed | tf_op | source)
XLA Modules:
  0.0 293.9 jit_solution(5636809482107577958)
XLA Ops:
  15.1 23.3 %psum.7 = f32[4,2]{0,1:T(2,128)S(1)} all-reduce(f32[4,2]{0,1:T(2,128)S(1)} %pad_maximum_fusion.9), channel_id=1, replica_groups=mesh['rep'=2,'atom'=8,'dir'=2] {'atom'}, use_global_device_ids=true, to_apply=%region_10.11 | all-reduce | flops 8 | bytes 64 | tf_op jit(solution)/shard_map/psum | solution.py:310
  42.1 11.2 %pass_one.6 = f32[8,12,32,128]{3,2,1,0:T(8,128)} custom-call(f32[3,4,1024]{2,1,0:T(4,128)} %slice.245.proj_ref, f32[16,1]{1,0:T(8,128)} %constant.189.node_ref, bf16[256,192]{1,0:T(8,128)(2,1)} %concatenate.78.coef_ref, f32[256,1024]{1,0:T(8,128)} %get-tuple-element.100.qt_ref, f32[256,1024]{1,0:T(8,128)} %get-tuple-element.75.kt_ref, ...), custom_call_target="tpu_custom_call" | custom-call | tf_op jit(solution)/shard_map/pass_one/pallas_call | solution.py:153
  53.3 11.3 %pass_one.5 = f32[8,12,32,128]{3,2,1,0:T(8,128)} custom-call(f32[3,4,1024]{2,1,0:T(4,128)} %slice.230.proj_ref, f32[16,1]{1,0:T(8,128)} %constant.189.node_ref, bf16[256,192]{1,0:T(8,128)(2,1)} %concatenate.78.coef_ref, f32[256,1024]{1,0:T(8,128)} %get-tuple-element.100.qt_ref, f32[256,1024]{1,0:T(8,128)} %get-tuple-element.75.kt_ref, ...), custom_call_target="tpu_custom_call" | custom-call | tf_op jit(solution)/shard_map/pass_one/pallas_call | solution.py:153
  64.6 11.2 %pass_one.4 = f32[8,12,32,128]{3,2,1,0:T(8,128)} custom-call(f32[3,4,1024]{2,1,0:T(4,128)} %slice.215.proj_ref, f32[16,1]{1,0:T(8,128)} %constant.189.node_ref, bf16[256,192]{1,0:T(8,128)(2,1)} %concatenate.78.coef_ref, f32[256,1024]{1,0:T(8,128)} %get-tuple-element.100.qt_ref, f32[256,1024]{1,0:T(8,128)} %get-tuple-element.75.kt_ref, ...), custom_call_target="tpu_custom_call" | custom-call | tf_op jit(solution)/shard_map/pass_one/pallas_call | solution.py:153
  75.8 3.2 %broadcast_multiply_fusion = (f32[8,12,32,128]{3,2,1,0:T(8,128)S(1)}, f32[8,12,32,128]{3,2,1,0:T(8,128)S(1)}, f32[8,12,32,128]{3,2,1,0:T(8,128)S(1)}) fusion(f32[8,12,32,128]{3,2,1,0:T(8,128)} %pass_one.6, f32[8,128]{1,0:T(8,128)S(1)} %bitcast.291, f32[8,12,32,128]{3,2,1,0:T(8,128)} %pass_one.5, f32[8,12,32,128]{3,2,1,0:T(8,128)} %pass_one.4), kind=kLoop, calls=%fused_computation.23 | loop fusion | flops 1179648 | bytes 9441280 | tf_op jit(solution)/shard_map/mul | solution.py:316
  86.0 8.5 %pass_one.7 = f32[8,8,32,128]{3,2,1,0:T(8,128)} custom-call(f32[2,4,1024]{2,1,0:T(4,128)} %slice.260.proj_ref, f32[16,1]{1,0:T(8,128)} %constant.189.node_ref, bf16[256,192]{1,0:T(8,128)(2,1)} %concatenate.78.coef_ref, f32[256,1024]{1,0:T(8,128)} %get-tuple-element.100.qt_ref, f32[256,1024]{1,0:T(8,128)} %get-tuple-element.75.kt_ref, ...), custom_call_target="tpu_custom_call" | custom-call | tf_op jit(solution)/shard_map/pass_one/pallas_call | solution.py:153
  94.5 2.4 broadcast_multiply_fusion.3
  101.6 2.0 copy.83
  103.6 2.0 copy.82
  106.3 2.8 fusion.5.rhs_ref
  113.4 2.1 collective-permute-start.20
  127.1 2.1 collective-permute-done.17
  131.4 2.9 collective-permute-done.50
  136.5 2.6 collective-permute-done.54
  143.9 2.5 collective-permute-start.6
  153.5 2.5 collective-permute-start.7
  160.7 2.2 collective-permute-done.61
  172.0 2.6 collective-permute-done.63
  195.8 15.0 %pass_two.4 = (f32[256,1024]{1,0:T(8,128)}, f32[256,1024]{1,0:T(8,128)}, f32[256,1024]{1,0:T(8,128)}) custom-call(s32[1]{0:T(128)} %bitcast.1.first_ref, f32[2,4,1024]{2,1,0:T(4,128)} %slice.260.proj_ref, f32[16,1]{1,0:T(8,128)} %constant.189.node_ref, ...), custom_call_target="tpu_custom_call", output_to_operand_aliasing={{0}: (7, {}), {1}: (8, {}), {2}: (9, {})} | custom-call | tf_op jit(solution)/shard_map/pass_two/pallas_call | solution.py:179
  219.3 20.2 %pass_two.5 = (f32[256,1024]{1,0:T(8,128)}, f32[256,1024]{1,0:T(8,128)}, f32[256,1024]{1,0:T(8,128)}) custom-call(s32[1]{0:T(128)} %bitcast.1.first_ref, f32[3,4,1024]{2,1,0:T(4,128)} %slice.245.proj_ref, f32[16,1]{1,0:T(8,128)} %constant.189.node_ref, ...), custom_call_target="tpu_custom_call", output_to_operand_aliasing={{0}: (7, {}), {1}: (8, {}), {2}: (9, {})} | custom-call | tf_op jit(solution)/shard_map/pass_two/pallas_call | solution.py:179
  240.5 20.2 %pass_two.6 = (f32[256,1024]{1,0:T(8,128)}, f32[256,1024]{1,0:T(8,128)}, f32[256,1024]{1,0:T(8,128)}) custom-call(s32[1]{0:T(128)} %bitcast.1.first_ref, f32[3,4,1024]{2,1,0:T(4,128)} %slice.230.proj_ref, f32[16,1]{1,0:T(8,128)} %constant.189.node_ref, ...), custom_call_target="tpu_custom_call", output_to_operand_aliasing={{0}: (7, {}), {1}: (8, {}), {2}: (9, {})} | custom-call | tf_op jit(solution)/shard_map/pass_two/pallas_call | solution.py:179
  261.7 20.5 %pass_two.7 = (f32[256,1024]{1,0:T(8,128)}, f32[256,1024]{1,0:T(8,128)}, f32[256,1024]{1,0:T(8,128)}) custom-call(s32[1]{0:T(128)} %bitcast.1.first_ref, f32[3,4,1024]{2,1,0:T(4,128)} %slice.215.proj_ref, f32[16,1]{1,0:T(8,128)} %constant.189.node_ref, ...), custom_call_target="tpu_custom_call", output_to_operand_aliasing={{0}: (7, {}), {1}: (8, {}), {2}: (9, {})} | custom-call | tf_op jit(solution)/shard_map/pass_two/pallas_call | solution.py:179
  282.8 2.3 collective-permute-done.66
  288.1 2.6 fusion.12
  (300 shorter events, 106.3 us)
Async XLA Ops:
  80.9 35.7 %collective-permute-start = (f16[6,32,128]{2,1,0:T(8,128)(2,1)}, f16[6,32,128]{2,1,0:T(8,128)(2,1)}, u32[]{:S(2)}, u32[]{:S(2)}) collective-permute-start(f16[6,32,128]{2,1,0:T(8,128)(2,1)} %get-tuple-element.62), channel_id=1, source_target_pairs={{0,4},{4,8},{8,12},{12,14},{14,10},{10,6},{6,2},{2,0},{1,5},{5,9},... | collective-permute-start | bytes 147464 | tf_op jit(solution)/shard_map/ppermute | solution.py:218
  80.9 37.6 %collective-permute-start.4 = (f16[6,32,128]{2,1,0:T(8,128)(2,1)}, f16[6,32,128]{2,1,0:T(8,128)(2,1)}, u32[]{:S(2)}, u32[]{:S(2)}) collective-permute-start(f16[6,32,128]{2,1,0:T(8,128)(2,1)} %get-tuple-element.63), channel_id=1, source_target_pairs={{4,0},{8,4},{12,8},{14,12},{10,14},{6,10},{2,6},{0,2},{5,1},{9,5},... | collective-permute-start | bytes 147464 | tf_op jit(solution)/shard_map/ppermute | solution.py:221
  83.6 36.1 %collective-permute-start.16 = (f16[6,32,128]{2,1,0:T(8,128)(2,1)}, f16[6,32,128]{2,1,0:T(8,128)(2,1)}, u32[]{:S(2)}, u32[]{:S(2)}) collective-permute-start(f16[6,32,128]{2,1,0:T(8,128)(2,1)} %get-tuple-element.54), channel_id=1, source_target_pairs={{0,4},{4,8},{8,12},{12,14},{14,10},{10,6},{6,2},{2,0},{1,5},{5,9},... | collective-permute-start | bytes 147464 | tf_op jit(solution)/shard_map/ppermute | solution.py:218
  98.4 14.9 %collective-permute-start.48 = (f16[4,32,128]{2,1,0:T(8,128)(2,1)}, f16[4,32,128]{2,1,0:T(8,128)(2,1)}, u32[]{:S(2)}, u32[]{:S(2)}) collective-permute-start(f16[4,32,128]{2,1,0:T(8,128)(2,1)} %get-tuple-element.70), channel_id=1, source_target_pairs={{0,4},{4,8},{8,12},{12,14},{14,10},{10,6},{6,2},{2,0},{1,5},{5,9},... | collective-permute-start | bytes 98312 | tf_op jit(solution)/shard_map/ppermute | solution.py:218
  98.4 17.0 %collective-permute-start.52 = (f16[4,32,128]{2,1,0:T(8,128)(2,1)S(1)}, f16[4,32,128]{2,1,0:T(8,128)(2,1)}, u32[]{:S(2)}, u32[]{:S(2)}) collective-permute-start(f16[4,32,128]{2,1,0:T(8,128)(2,1)S(1)} %get-tuple-element.71), channel_id=1, source_target_pairs={{4,0},{8,4},{12,8},{14,12},{10,14},{6,10},{2,6},{0,2},{5,1},{9,5},... | collective-permute-start | bytes 98312 | tf_op jit(solution)/shard_map/ppermute | solution.py:221
  113.4 8.3 %collective-permute-start.20 = (f16[6,32,128]{2,1,0:T(8,128)(2,1)}, f16[6,32,128]{2,1,0:T(8,128)(2,1)S(1)}, u32[]{:S(2)}, u32[]{:S(2)}) collective-permute-start(f16[6,32,128]{2,1,0:T(8,128)(2,1)} %get-tuple-element.55), channel_id=1, source_target_pairs={{4,0},{8,4},{12,8},{14,12},{10,14},{6,10},{2,6},{0,2},{5,1},{9,5},... | collective-permute-start | bytes 147464 | tf_op jit(solution)/shard_map/ppermute | solution.py:221
  119.7 9.7 %collective-permute-start.53 = (f16[8,32,128]{2,1,0:T(8,128)(2,1)S(1)}, f16[8,32,128]{2,1,0:T(8,128)(2,1)S(1)}, u32[]{:S(2)}, u32[]{:S(2)}) collective-permute-start(f16[8,32,128]{2,1,0:T(8,128)(2,1)S(1)} %pad_maximum_fusion.7), channel_id=1, source_target_pairs={{4,0},{8,4},{12,8},{14,12},{10,14},{6,10},{2,6},{0,2},{5,1},{9,5},... | collective-permute-start | bytes 196616 | tf_op jit(solution)/shard_map/ppermute | solution.py:221
  122.7 16.4 %collective-permute-start.5 = (f16[12,32,128]{2,1,0:T(8,128)(2,1)S(1)}, f16[12,32,128]{2,1,0:T(8,128)(2,1)S(1)}, u32[]{:S(2)}, u32[]{:S(2)}) collective-permute-start(f16[12,32,128]{2,1,0:T(8,128)(2,1)S(1)} %pad_maximum_fusion.1), channel_id=1, source_target_pairs={{4,0},{8,4},{12,8},{14,12},{10,14},{6,10},{2,6},{0,2},{5,1},{9,5},... | collective-permute-start | bytes 294920 | tf_op jit(solution)/shard_map/ppermute | solution.py:221
  124.9 16.2 %collective-permute-start.21 = (f16[12,32,128]{2,1,0:T(8,128)(2,1)S(1)}, f16[12,32,128]{2,1,0:T(8,128)(2,1)S(1)}, u32[]{:S(2)}, u32[]{:S(2)}) collective-permute-start(f16[12,32,128]{2,1,0:T(8,128)(2,1)S(1)} %pad_maximum_fusion.3), channel_id=1, source_target_pairs={{4,0},{8,4},{12,8},{14,12},{10,14},{6,10},{2,6},{0,2},{5,1},{9,5},... | collective-permute-start | bytes 294920 | tf_op jit(solution)/shard_map/ppermute | solution.py:221
  129.4 17.0 %collective-permute-start.37 = (f16[12,32,128]{2,1,0:T(8,128)(2,1)S(1)}, f16[12,32,128]{2,1,0:T(8,128)(2,1)S(1)}, u32[]{:S(2)}, u32[]{:S(2)}) collective-permute-start(f16[12,32,128]{2,1,0:T(8,128)(2,1)S(1)} %pad_maximum_fusion.5), channel_id=1, source_target_pairs={{4,0},{8,4},{12,8},{14,12},{10,14},{6,10},{2,6},{0,2},{5,1},{9,5},... | collective-permute-start | bytes 294920 | tf_op jit(solution)/shard_map/ppermute | solution.py:221
  140.5 8.1 %collective-permute-start.51 = (f16[8,32,128]{2,1,0:T(8,128)(2,1)S(1)}, f16[8,32,128]{2,1,0:T(8,128)(2,1)S(1)}, u32[]{:S(2)}, u32[]{:S(2)}) collective-permute-start(f16[8,32,128]{2,1,0:T(8,128)(2,1)S(1)} %get-tuple-element.66), channel_id=1, source_target_pairs={{0,4},{4,8},{8,12},{12,14},{14,10},{10,6},{6,2},{2,0},{1,5},{5,9},... | collective-permute-start | bytes 196616 | tf_op jit(solution)/shard_map/ppermute | solution.py:218
  146.5 9.5 %collective-permute-start.3 = (f16[12,32,128]{2,1,0:T(8,128)(2,1)S(1)}, f16[12,32,128]{2,1,0:T(8,128)(2,1)S(1)}, u32[]{:S(2)}, u32[]{:S(2)}) collective-permute-start(f16[12,32,128]{2,1,0:T(8,128)(2,1)S(1)} %get-tuple-element.58), channel_id=1, source_target_pairs={{0,4},{4,8},{8,12},{12,14},{14,10},{10,6},{6,2},{2,0},{1,5},{5,9},... | collective-permute-start | bytes 294920 | tf_op jit(solution)/shard_map/ppermute | solution.py:218
  148.6 11.5 %collective-permute-start.19 = (f16[12,32,128]{2,1,0:T(8,128)(2,1)S(1)}, f16[12,32,128]{2,1,0:T(8,128)(2,1)S(1)}, u32[]{:S(2)}, u32[]{:S(2)}) collective-permute-start(f16[12,32,128]{2,1,0:T(8,128)(2,1)S(1)} %get-tuple-element.50), channel_id=1, source_target_pairs={{0,4},{4,8},{8,12},{12,14},{14,10},{10,6},{6,2},{2,0},{1,5},{5,9},... | collective-permute-start | bytes 294920 | tf_op jit(solution)/shard_map/ppermute | solution.py:218
  156.0 13.9 %collective-permute-start.35 = (f16[12,32,128]{2,1,0:T(8,128)(2,1)S(1)}, f16[12,32,128]{2,1,0:T(8,128)(2,1)S(1)}, u32[]{:S(2)}, u32[]{:S(2)}) collective-permute-start(f16[12,32,128]{2,1,0:T(8,128)(2,1)S(1)} %get-tuple-element.42), channel_id=1, source_target_pairs={{0,4},{4,8},{8,12},{12,14},{14,10},{10,6},{6,2},{2,0},{1,5},{5,9},... | collective-permute-start | bytes 294920 | tf_op jit(solution)/shard_map/ppermute | solution.py:218
  156.1 8.9 %collective-permute-start.23 = (f16[12,32,128]{2,1,0:T(8,128)(2,1)S(1)}, f16[12,32,128]{2,1,0:T(8,128)(2,1)S(1)}, u32[]{:S(2)}, u32[]{:S(2)}) collective-permute-start(f16[12,32,128]{2,1,0:T(8,128)(2,1)S(1)} %fusion.21), channel_id=1, source_target_pairs={{4,0},{8,4},{12,8},{14,12},{10,14},{6,10},{2,6},{0,2},{5,1},{9,5},... | collective-permute-start | bytes 294920 | tf_op jit(solution)/shard_map/ppermute | solution.py:221
  160.2 11.5 %collective-permute-start.39 = (f16[12,32,128]{2,1,0:T(8,128)(2,1)S(1)}, f16[12,32,128]{2,1,0:T(8,128)(2,1)S(1)}, u32[]{:S(2)}, u32[]{:S(2)}) collective-permute-start(f16[12,32,128]{2,1,0:T(8,128)(2,1)S(1)} %fusion.14), channel_id=1, source_target_pairs={{4,0},{8,4},{12,8},{14,12},{10,14},{6,10},{2,6},{0,2},{5,1},{9,5},... | collective-permute-start | bytes 294920 | tf_op jit(solution)/shard_map/ppermute | solution.py:221
  165.0 11.7 %collective-permute-start.12 = (bf16[12,32,128]{2,1,0:T(8,128)(2,1)S(1)}, bf16[12,32,128]{2,1,0:T(8,128)(2,1)S(1)}, u32[]{:S(2)}, u32[]{:S(2)}) collective-permute-start(bf16[12,32,128]{2,1,0:T(8,128)(2,1)S(1)} %fusion.33), channel_id=1, source_target_pairs={{4,0},{8,4},{12,8},{14,12},{10,14},{6,10},{2,6},{0,2},{5,1},{9,5},... | collective-permute-start | bytes 294920 | tf_op jit(solution)/shard_map/ppermute | solution.py:221
  167.9 9.9 %collective-permute-start.8 = (bf16[12,32,128]{2,1,0:T(8,128)(2,1)S(1)}, bf16[12,32,128]{2,1,0:T(8,128)(2,1)S(1)}, u32[]{:S(2)}, u32[]{:S(2)}) collective-permute-start(bf16[12,32,128]{2,1,0:T(8,128)(2,1)S(1)} %fusion.33), channel_id=1, source_target_pairs={{0,4},{4,8},{8,12},{12,14},{14,10},{10,6},{6,2},{2,0},{1,5},{5,9},... | collective-permute-start | bytes 294920 | tf_op jit(solution)/shard_map/ppermute | solution.py:218
  169.6 9.2 %collective-permute-start.28 = (bf16[12,32,128]{2,1,0:T(8,128)(2,1)S(1)}, bf16[12,32,128]{2,1,0:T(8,128)(2,1)S(1)}, u32[]{:S(2)}, u32[]{:S(2)}) collective-permute-start(bf16[12,32,128]{2,1,0:T(8,128)(2,1)S(1)} %fusion.26), channel_id=1, source_target_pairs={{4,0},{8,4},{12,8},{14,12},{10,14},{6,10},{2,6},{0,2},{5,1},{9,5},... | collective-permute-start | bytes 294920 | tf_op jit(solution)/shard_map/ppermute | solution.py:221
  187.0 23.8 %collective-permute-start.26 = (bf16[12,32,128]{2,1,0:T(8,128)(2,1)S(1)}, bf16[12,32,128]{2,1,0:T(8,128)(2,1)S(1)}, u32[]{:S(2)}, u32[]{:S(2)}) collective-permute-start(bf16[12,32,128]{2,1,0:T(8,128)(2,1)S(1)} %collective-permute-done.25), channel_id=1, source_target_pairs={{0,4},{4,8},{8,12},{12,14},{14,10},{10,6},{6,2},{2,0},{1,5},{5,9},... | collective-permute-start | bytes 294920 | tf_op jit(solution)/shard_map/ppermute | solution.py:218
  188.1 23.9 %collective-permute-start.46 = (bf16[12,32,128]{2,1,0:T(8,128)(2,1)S(1)}, bf16[12,32,128]{2,1,0:T(8,128)(2,1)S(1)}, u32[]{:S(2)}, u32[]{:S(2)}) collective-permute-start(bf16[12,32,128]{2,1,0:T(8,128)(2,1)S(1)} %collective-permute-done.45), channel_id=1, source_target_pairs={{4,0},{8,4},{12,8},{14,12},{10,14},{6,10},{2,6},{0,2},{5,1},{9,5},... | collective-permute-start | bytes 294920 | tf_op jit(solution)/shard_map/ppermute | solution.py:221
  189.1 23.9 %collective-permute-start.42 = (bf16[12,32,128]{2,1,0:T(8,128)(2,1)S(1)}, bf16[12,32,128]{2,1,0:T(8,128)(2,1)S(1)}, u32[]{:S(2)}, u32[]{:S(2)}) collective-permute-start(bf16[12,32,128]{2,1,0:T(8,128)(2,1)S(1)} %collective-permute-done.41), channel_id=1, source_target_pairs={{0,4},{4,8},{8,12},{12,14},{14,10},{10,6},{6,2},{2,0},{1,5},{5,9},... | collective-permute-start | bytes 294920 | tf_op jit(solution)/shard_map/ppermute | solution.py:218
  190.1 24.0 %collective-permute-start.15 = (bf16[6,32,128]{2,1,0:T(8,128)(2,1)S(1)}, bf16[6,32,128]{2,1,0:T(8,128)(2,1)S(1)}, u32[]{:S(2)}, u32[]{:S(2)}) collective-permute-start(bf16[6,32,128]{2,1,0:T(8,128)(2,1)S(1)} %slice.275), channel_id=1, source_target_pairs={{4,0},{8,4},{12,8},{14,12},{10,14},{6,10},{2,6},{0,2},{5,1},{9,5},... | collective-permute-start | bytes 147464 | tf_op jit(solution)/shard_map/ppermute | solution.py:221
  191.2 23.9 %collective-permute-start.11 = (bf16[6,32,128]{2,1,0:T(8,128)(2,1)S(1)}, bf16[6,32,128]{2,1,0:T(8,128)(2,1)S(1)}, u32[]{:S(2)}, u32[]{:S(2)}) collective-permute-start(bf16[6,32,128]{2,1,0:T(8,128)(2,1)S(1)} %slice.274), channel_id=1, source_target_pairs={{0,4},{4,8},{8,12},{12,14},{14,10},{10,6},{6,2},{2,0},{1,5},{5,9},... | collective-permute-start | bytes 147464 | tf_op jit(solution)/shard_map/ppermute | solution.py:218
  (66 other events, 400.2 us)
